TPU v7x, 32 devices: a whole 2x2x4 slice. The times are simulated.
32 devices in a mesh: dp: 2 (over x), ind: 4 (over z), probe: 4 (over y, core).
Axes of the slice: x: 2, y: 2, z: 4, core: 2. Of those that a mesh axis runs over, the one named last changes fastest.
Arguments:
- data_x: bfloat16 [16, 1024], P(None, 'dp'), may hold values from -6 to 6
- inducing_z: bfloat16 [16, 65536], P(None, 'ind'), may hold values from -6 to 6
- lengthscale: float32 [16], replicated, may hold values from 1.5 to 3
- noise_var: float32 [1], replicated, may hold values from 0.5 to 2
- solves: bfloat16 [32, 65536], P('probe', 'ind'), may hold values from -0.09375 to 0.09375
- probe_signs: int32 [32, 65536], P('probe', 'ind'), may hold values 0 or 1
Outputs:
- grad_z: float32 [16, 65536], P(None, 'ind')
All inputs are finite; a program needn't handle non-finite values. No bound on the sum of `probe_signs` on one device may be relied on, other than what follows from the above.
Results may differ from a plain program's by a relative error of at most 0.0095.
Values may be sent and summed in bfloat16 or wider, within the bound.
No kernel may reach another device: no remote copies, remote signals or barrier semaphores. Data moves between devices by JAX's collectives and lax.ppermute only.
A program may use at most 64 MiB of HBM per device.

v0:
```python
import jax
import jax.numpy as jnp
from jax import lax
from jax.sharding import PartitionSpec as P

P_SIZE = 32


def kernel_block(x_scaled, x_square, z_scaled, z_square):
    cross = lax.dot_general(
        x_scaled, z_scaled, (((0,), (0,)), ((), ())), preferred_element_type=jnp.float32
    )
    dist = x_square[:, None] + z_square[None, :] - 2.0 * cross
    return jnp.exp(-0.5 * dist).astype(jnp.bfloat16)


def on_device(data_x, inducing_z, lengthscale, noise_var, solves, probe_signs):
    probe_vals = (2 * probe_signs - 1).astype(jnp.bfloat16)
    stacked = jnp.concatenate([solves, probe_vals], axis=0)
    half_rows = stacked.shape[0] // 2
    inverse = 1.0 / lengthscale
    x_scaled = (data_x.astype(jnp.float32) * inverse[:, None]).astype(jnp.bfloat16)
    z_scaled = (inducing_z.astype(jnp.float32) * inverse[:, None]).astype(jnp.bfloat16)
    x_wide = x_scaled.astype(jnp.float32)
    z_wide = z_scaled.astype(jnp.float32)
    x_square = jnp.sum(x_wide * x_wide, axis=0)
    z_square = jnp.sum(z_wide * z_wide, axis=0)
    total_cols = z_scaled.shape[1]
    block_cols = min(2048, total_cols)
    blocks_count = total_cols // block_cols
    rows_count = x_scaled.shape[1]

    def first_pass(col_index, totals):
        start = col_index * block_cols
        z_part = lax.dynamic_slice_in_dim(z_scaled, start, block_cols, 1)
        zsq_part = lax.dynamic_slice_in_dim(z_square, start, block_cols, 0)
        kern = kernel_block(x_scaled, x_square, z_part, zsq_part)
        stack_part = lax.dynamic_slice_in_dim(stacked, start, block_cols, 1)
        return totals + lax.dot_general(
            stack_part, kern, (((1,), (1,)), ((), ())), preferred_element_type=jnp.float32
        )

    partial_proj = lax.fori_loop(
        0, blocks_count, first_pass, jnp.zeros((2 * half_rows, rows_count), jnp.float32)
    )
    projections = lax.psum(partial_proj.astype(jnp.bfloat16), "ind")
    swapped = jnp.concatenate([projections[half_rows:], projections[:half_rows]], axis=0)

    def second_pass(col_index, result):
        start = col_index * block_cols
        z_part = lax.dynamic_slice_in_dim(z_scaled, start, block_cols, 1)
        zsq_part = lax.dynamic_slice_in_dim(z_square, start, block_cols, 0)
        kern = kernel_block(x_scaled, x_square, z_part, zsq_part)
        stack_part = lax.dynamic_slice_in_dim(stacked, start, block_cols, 1)
        coef = lax.dot_general(
            swapped, stack_part, (((0,), (0,)), ((), ())), preferred_element_type=jnp.float32
        )
        weighted = (kern.astype(jnp.float32) * coef).astype(jnp.bfloat16)
        moment = jnp.dot(data_x, weighted, preferred_element_type=jnp.float32)
        row_total = jnp.sum(weighted, axis=0, dtype=jnp.float32)
        z_raw = lax.dynamic_slice_in_dim(inducing_z, start, block_cols, 1).astype(jnp.float32)
        return lax.dynamic_update_slice_in_dim(
            result, moment - z_raw * row_total[None, :], start, 1
        )

    partial_grad = lax.fori_loop(
        0, blocks_count, second_pass, jnp.zeros((x_scaled.shape[0], total_cols), jnp.float32)
    )
    summed = lax.psum(partial_grad, ("dp", "probe"))
    factor = inverse * inverse / (noise_var[0] * P_SIZE)
    return summed * factor[:, None]


def solution(mesh):
    return jax.shard_map(
        on_device,
        mesh=mesh,
        in_specs=(P(None, "dp"), P(None, "ind"), P(), P(), P("probe", "ind"), P("probe", "ind")),
        out_specs=P(None, "ind"),
        check_vma=False,
    )
```

profile of v0, /device:TPU:0, one launch (start us, length us, event | category | flops | bytes accessed | tf_op | source)
XLA Modules:
  0.0 134.0 jit_solution(3839862775014209474)
XLA Ops:
  6.5 0.0 copy-start.2
  6.5 0.0 all-reduce.2.cloned.1.call-start
  7.2 1.1 add_convert_fusion
  8.3 0.7 multiply_divide_fusion
  9.0 0.8 multiply_reduce_fusion.1
  9.8 1.4 %multiply_reduce_fusion = (f32[16384]{0:T(1024)S(1)}, bf16[16,16384]{1,0:T(8,128)(2,1)S(1)}) fusion(f32[16]{0:T(128)S(1)} %get-tuple-element.359, bf16[16,16384]{1,0:T(8,128)(2,1)} %param.11), kind=kLoop, calls=%fused_computation.25 | loop fusion | flops 1556480 | bytes 1114176 | tf_op jit(solution)/shard_map/reduce_sum | solution.py:27
  11.2 0.0 copy-done.2
  11.3 0.0 copy-start.1
  11.3 11.8 %while.28 = (s32[]{:T(128)}, f32[16,512]{1,0:T(8,128)S(1)}, bf16[16,16384]{1,0:T(8,128)(2,1)S(1)}, f32[512]{0:T(512)S(1)}, f32[16384]{0:T(1024)S(1)}, /*index=5*...) while((s32[]{:T(128)}, f32[16,512]{1,0:T(8,128)S(1)}, ...), condition=%wide.region_3.0_spmd.clone, body=%wide.region_2.0_spmd.clone.sunk | while | flops 72368136 | bytes 241328 | solution.py:43
  11.3 1.5 %fusion.49 = f32[16,512]{1,0:T(8,128)S(1)} fusion(bf16[16,512]{1,0:T(8,128)(2,1)S(1)} %get-tuple-element.504, f32[2048]{0:T(1024)S(1)} %dynamic_slice.77, f32[512]{0:T(512)S(1)} %get-tuple-element.501, bf16[16,16384]{1,0:T(8,128)(2,1)S(1)} %get-tuple-element.503, s32[]{:T(128)S(6)} %select_n.24, bf16[16,16384]{1,0:T(8,128)(2,1)S(1)} %get-tuple-element.500, ...), kind=kOutput, calls=%fused_computation.19.clone.1 | convolution fusion | flops 72368128 | bytes 224768 | tf_op jit(solution)/shard_map/while/body/eval_jaxpr/dot_general | solution.py:39
  12.8 1.5 %fusion.49 = f32[16,512]{1,0:T(8,128)S(1)} fusion(bf16[16,512]{1,0:T(8,128)(2,1)S(1)} %get-tuple-element.504, f32[2048]{0:T(1024)S(1)} %dynamic_slice.77, f32[512]{0:T(512)S(1)} %get-tuple-element.501, bf16[16,16384]{1,0:T(8,128)(2,1)S(1)} %get-tuple-element.503, s32[]{:T(128)S(6)} %select_n.24, bf16[16,16384]{1,0:T(8,128)(2,1)S(1)} %get-tuple-element.500, ...), kind=kOutput, calls=%fused_computation.19.clone.1 | convolution fusion | flops 72368128 | bytes 224768 | tf_op jit(solution)/shard_map/while/body/eval_jaxpr/dot_general | solution.py:39
  14.2 1.5 %fusion.49 = f32[16,512]{1,0:T(8,128)S(1)} fusion(bf16[16,512]{1,0:T(8,128)(2,1)S(1)} %get-tuple-element.504, f32[2048]{0:T(1024)S(1)} %dynamic_slice.77, f32[512]{0:T(512)S(1)} %get-tuple-element.501, bf16[16,16384]{1,0:T(8,128)(2,1)S(1)} %get-tuple-element.503, s32[]{:T(128)S(6)} %select_n.24, bf16[16,16384]{1,0:T(8,128)(2,1)S(1)} %get-tuple-element.500, ...), kind=kOutput, calls=%fused_computation.19.clone.1 | convolution fusion | flops 72368128 | bytes 224768 | tf_op jit(solution)/shard_map/while/body/eval_jaxpr/dot_general | solution.py:39
  15.7 1.5 %fusion.49 = f32[16,512]{1,0:T(8,128)S(1)} fusion(bf16[16,512]{1,0:T(8,128)(2,1)S(1)} %get-tuple-element.504, f32[2048]{0:T(1024)S(1)} %dynamic_slice.77, f32[512]{0:T(512)S(1)} %get-tuple-element.501, bf16[16,16384]{1,0:T(8,128)(2,1)S(1)} %get-tuple-element.503, s32[]{:T(128)S(6)} %select_n.24, bf16[16,16384]{1,0:T(8,128)(2,1)S(1)} %get-tuple-element.500, ...), kind=kOutput, calls=%fused_computation.19.clone.1 | convolution fusion | flops 72368128 | bytes 224768 | tf_op jit(solution)/shard_map/while/body/eval_jaxpr/dot_general | solution.py:39
  17.2 1.5 %fusion.49 = f32[16,512]{1,0:T(8,128)S(1)} fusion(bf16[16,512]{1,0:T(8,128)(2,1)S(1)} %get-tuple-element.504, f32[2048]{0:T(1024)S(1)} %dynamic_slice.77, f32[512]{0:T(512)S(1)} %get-tuple-element.501, bf16[16,16384]{1,0:T(8,128)(2,1)S(1)} %get-tuple-element.503, s32[]{:T(128)S(6)} %select_n.24, bf16[16,16384]{1,0:T(8,128)(2,1)S(1)} %get-tuple-element.500, ...), kind=kOutput, calls=%fused_computation.19.clone.1 | convolution fusion | flops 72368128 | bytes 224768 | tf_op jit(solution)/shard_map/while/body/eval_jaxpr/dot_general | solution.py:39
  18.7 1.5 %fusion.49 = f32[16,512]{1,0:T(8,128)S(1)} fusion(bf16[16,512]{1,0:T(8,128)(2,1)S(1)} %get-tuple-element.504, f32[2048]{0:T(1024)S(1)} %dynamic_slice.77, f32[512]{0:T(512)S(1)} %get-tuple-element.501, bf16[16,16384]{1,0:T(8,128)(2,1)S(1)} %get-tuple-element.503, s32[]{:T(128)S(6)} %select_n.24, bf16[16,16384]{1,0:T(8,128)(2,1)S(1)} %get-tuple-element.500, ...), kind=kOutput, calls=%fused_computation.19.clone.1 | convolution fusion | flops 72368128 | bytes 224768 | tf_op jit(solution)/shard_map/while/body/eval_jaxpr/dot_general | solution.py:39
  20.1 1.5 %fusion.49 = f32[16,512]{1,0:T(8,128)S(1)} fusion(bf16[16,512]{1,0:T(8,128)(2,1)S(1)} %get-tuple-element.504, f32[2048]{0:T(1024)S(1)} %dynamic_slice.77, f32[512]{0:T(512)S(1)} %get-tuple-element.501, bf16[16,16384]{1,0:T(8,128)(2,1)S(1)} %get-tuple-element.503, s32[]{:T(128)S(6)} %select_n.24, bf16[16,16384]{1,0:T(8,128)(2,1)S(1)} %get-tuple-element.500, ...), kind=kOutput, calls=%fused_computation.19.clone.1 | convolution fusion | flops 72368128 | bytes 224768 | tf_op jit(solution)/shard_map/while/body/eval_jaxpr/dot_general | solution.py:39
  21.6 1.5 %fusion.49 = f32[16,512]{1,0:T(8,128)S(1)} fusion(bf16[16,512]{1,0:T(8,128)(2,1)S(1)} %get-tuple-element.504, f32[2048]{0:T(1024)S(1)} %dynamic_slice.77, f32[512]{0:T(512)S(1)} %get-tuple-element.501, bf16[16,16384]{1,0:T(8,128)(2,1)S(1)} %get-tuple-element.503, s32[]{:T(128)S(6)} %select_n.24, bf16[16,16384]{1,0:T(8,128)(2,1)S(1)} %get-tuple-element.500, ...), kind=kOutput, calls=%fused_computation.19.clone.1 | convolution fusion | flops 72368128 | bytes 224768 | tf_op jit(solution)/shard_map/while/body/eval_jaxpr/dot_general | solution.py:39
  23.1 20.5 %psum.14 = bf16[16,512]{1,0:T(8,128)(2,1)S(1)} all-reduce(bf16[16,512]{1,0:T(8,128)(2,1)S(1)} %convert_element_type.73), channel_id=1, replica_groups=mesh['dp'=2,'ind'=4,'probe'=4] {'ind'}, use_global_device_ids=true, to_apply=%region_4.0 | all-reduce | flops 8192 | bytes 32768 | tf_op jit(solution)/shard_map/psum | solution.py:46
  43.6 0.1 broadcast_in_dim.24
  43.7 0.0 copy-done.1
  43.7 25.0 %while.27 = (s32[]{:T(128)}, f32[16,16384]{1,0:T(8,128)S(1)}, f32[512]{0:T(512)S(1)}, f32[16384]{0:T(1024)S(1)}, bf16[16,16384]{1,0:T(8,128)(2,1)S(1)}, /*index=...) while((s32[]{:T(128)}, f32[16,16384]{1,0:T(8,128)S(1)}, ...), condition=%wide.region_7.0_spmd, body=%wide.region_5.0_spmd.sunk | while | flops 111245312 | bytes 8808643 | solution.py:66
  43.8 1.1 fusion.44
  44.9 0.8 convert_reduce_fusion.2
  45.6 1.2 fusion.45
  46.9 1.1 fusion.44
  48.0 0.8 convert_reduce_fusion.2
  48.8 1.2 fusion.45
  50.0 1.1 fusion.44
  51.1 0.8 convert_reduce_fusion.2
  51.9 1.2 fusion.45
  53.1 1.1 fusion.44
  54.2 0.8 convert_reduce_fusion.2
  55.0 1.2 fusion.45
  56.2 1.1 fusion.44
  57.4 0.8 convert_reduce_fusion.2
  58.1 1.2 fusion.45
  59.4 1.1 fusion.44
  60.5 0.8 convert_reduce_fusion.2
  61.2 1.2 fusion.45
  62.5 1.1 fusion.44
  63.6 0.8 convert_reduce_fusion.2
  64.4 1.2 fusion.45
  65.6 1.1 fusion.44
  66.7 0.8 convert_reduce_fusion.2
  67.5 1.2 fusion.45
  68.7 0.0 copy-start
  68.7 1.0 copy-done
  69.7 0.0 all-reduce.2.cloned.1.call-update
  69.7 55.1 %all-reduce.2.cloned.1.call-done = f32[16,16384]{1,0:T(8,128)} async-done(((f32[16,16384]{1,0:T(8,128)}), f32[16,16384]{1,0:T(8,128)}) %all-reduce.2.cloned.1.call-update) | async-done | bytes 1048592 | tf_op jit(solution)/shard_map/psum | solution.py:69
  124.8 2.3 %broadcast_multiply_fusion = f32[16,16384]{1,0:T(8,128)} fusion(f32[16,16384]{1,0:T(8,128)} %all-reduce.2.cloned.1.call-done, f32[16]{0:T(128)S(1)} %get-tuple-element.358), kind=kLoop, calls=%fused_computation.28 | loop fusion | flops 262144 | bytes 2097216 | tf_op jit(solution)/shard_map/mul | solution.py:71
  (21 shorter events, 0.1 us)
Async XLA Ops:
  6.5 4.7 %copy-start.2 = (bf16[8,16384]{1,0:T(8,128)(2,1)S(1)}, bf16[8,16384]{1,0:T(8,128)(2,1)}, u32[]{:S(2)}) copy-start(bf16[8,16384]{1,0:T(8,128)(2,1)} %param.14) | copy-start | bytes 786436
  6.5 118.3 %all-reduce.2.cloned.1.call-start = ((), (), s32[]{:S(2)}) async-start(), calls=%async_computation | async-start | bytes 2097152 | tf_op jit(solution)/shard_map/psum | solution.py:69
  11.3 32.4 %copy-start.1 = (bf16[16,512]{1,0:T(8,128)(2,1)S(1)}, bf16[16,512]{1,0:T(8,128)(2,1)}, u32[]{:S(2)}) copy-start(bf16[16,512]{1,0:T(8,128)(2,1)} %param.10) | copy-start | bytes 49156
  68.7 1.0 copy-start
Sparse Core Ops, SparseCore 0:
  69.9 54.8 all-reduce.1
where the time goes:
time: 135 us; the launch traced here: 134 us
  waiting for transfers between devices  55.1 us (41%)
  matrix products  36.6 us (27%)
  blocking collectives  20.5 us (15%)
  between operations  14.1 us (10%)
  other arithmetic  6.35 us (5%)
    psum x1, waiting for transfers between devices, on_device(): summed = lax.psum(partial_grad, ('dp', 'probe'))  55.1 us
    psum x1, blocking collectives, on_device(): projections = lax.psum(partial_proj.astype(jnp.bfloat16), 'ind')  20.5 us
    dot_general x8, matrix products, first_pass(): lax.dot_general(stack_part, kern, (((1,), (1,)), ((), ())), preferred_ele...  11.8 us
    dot_general x8, matrix products, second_pass(): moment = jnp.dot(data_x, weighted, preferred_element_type=jnp.float32)  9.92 us
    dot_general x8, matrix products, kernel_block(): lax.dot_general(x_scaled, z_scaled, (((0,), (0,)), ((), ())), preferred_e...  8.83 us
    dot_general x8, matrix products, second_pass(): lax.dot_general(swapped, stack_part, (((0,), (0,)), ((), ())), preferred_...  6.1 us
  transfers between devices with their start and end apart: 1, of which 1 were waited for; matrix products, arithmetic and copies ran while one was open for 0% of the time, Pallas kernels for 0%

commit v1 on v0

--- a/solution.py
+++ b/solution.py
@@ -66,7 +66,7 @@
     partial_grad = lax.fori_loop(
         0, blocks_count, second_pass, jnp.zeros((x_scaled.shape[0], total_cols), jnp.float32)
     )
-    summed = lax.psum(partial_grad, ("dp", "probe"))
+    summed = lax.psum(lax.psum(partial_grad, "probe"), "dp")
     factor = inverse * inverse / (noise_var[0] * P_SIZE)
     return summed * factor[:, None]
 

time: 135 us -> 157 us (1.16)
  waiting for transfers between devices: 55.1 us -> 77.5 us
    psum x1 -> x2, waiting for transfers between devices: 55.1 us -> 77.5 us  [on_device(): summed = lax.psum(lax.psum(partial_grad, 'probe'), 'dp')]
  transfers between devices with their start and end apart: 1 -> 2, of which waited for: 1 -> 2; matrix products, arithmetic and copies ran while one was open for 0% -> 0% of each run, Pallas kernels for 0% -> 0%
where the time goes in v1:
time: 157 us; the launch traced here: 156 us
  waiting for transfers between devices  77.5 us (49%)
  matrix products  36.6 us (23%)
  blocking collectives  20.5 us (13%)
  between operations  14.2 us (9%)
  other arithmetic  6.35 us (4%)
    psum x2, waiting for transfers between devices, on_device(): summed = lax.psum(lax.psum(partial_grad, 'probe'), 'dp')  77.5 us
    psum x1, blocking collectives, on_device(): projections = lax.psum(partial_proj.astype(jnp.bfloat16), 'ind')  20.5 us
    dot_general x8, matrix products, first_pass(): lax.dot_general(stack_part, kern, (((1,), (1,)), ((), ())), preferred_ele...  11.8 us
    dot_general x8, matrix products, second_pass(): moment = jnp.dot(data_x, weighted, preferred_element_type=jnp.float32)  9.92 us
    dot_general x8, matrix products, kernel_block(): lax.dot_general(x_scaled, z_scaled, (((0,), (0,)), ((), ())), preferred_e...  8.83 us
    dot_general x8, matrix products, second_pass(): lax.dot_general(swapped, stack_part, (((0,), (0,)), ((), ())), preferred_...  6.1 us
  transfers between devices with their start and end apart: 2, of which 2 were waited for; matrix products, arithmetic and copies ran while one was open for 0% of the time, Pallas kernels for 0%

profile of v1, /device:TPU:0, one launch (start us, length us, event | category | flops | bytes accessed | tf_op | source)
XLA Modules:
  0.0 156.4 jit_solution(9150705907351827267)
XLA Ops:
  6.5 0.0 copy-start.2
  6.5 0.0 all-reduce.3.cloned.1.call-start
  7.2 1.1 add_convert_fusion
  8.3 0.7 multiply_divide_fusion
  9.0 0.8 multiply_reduce_fusion.1
  9.8 1.4 multiply_reduce_fusion
  11.2 0.0 copy-done.2
  11.3 0.0 copy-start.1
  11.3 11.8 %while.28 = (s32[]{:T(128)}, f32[16,512]{1,0:T(8,128)S(1)}, bf16[16,16384]{1,0:T(8,128)(2,1)S(1)}, f32[512]{0:T(512)S(1)}, f32[16384]{0:T(1024)S(1)}, /*index=5*...) while((s32[]{:T(128)}, f32[16,512]{1,0:T(8,128)S(1)}, ...), condition=%wide.region_3.0_spmd.clone, body=%wide.region_2.0_spmd.clone.sunk | while | flops 72368136 | bytes 241328 | solution.py:43
  11.3 1.5 fusion.49
  12.8 1.5 fusion.49
  14.2 1.5 fusion.49
  15.7 1.5 fusion.49
  17.2 1.5 fusion.49
  18.7 1.5 fusion.49
  20.1 1.5 fusion.49
  21.6 1.5 fusion.49
  23.1 20.5 %psum.21 = bf16[16,512]{1,0:T(8,128)(2,1)S(1)} all-reduce(bf16[16,512]{1,0:T(8,128)(2,1)S(1)} %convert_element_type.73), channel_id=1, replica_groups=mesh['dp'=2,'ind'=4,'probe'=4] {'ind'}, use_global_device_ids=true, to_apply=%region_4.0 | all-reduce | flops 8192 | bytes 32768 | tf_op jit(solution)/shard_map/psum | solution.py:46
  43.6 0.1 broadcast_in_dim.24
  43.7 0.0 copy-done.1
  43.7 25.0 %while.27 = (s32[]{:T(128)}, f32[16,16384]{1,0:T(8,128)S(1)}, f32[512]{0:T(512)S(1)}, f32[16384]{0:T(1024)S(1)}, bf16[16,16384]{1,0:T(8,128)(2,1)S(1)}, /*index=...) while((s32[]{:T(128)}, f32[16,16384]{1,0:T(8,128)S(1)}, ...), condition=%wide.region_7.0_spmd, body=%wide.region_5.0_spmd.sunk | while | flops 111245312 | bytes 8808643 | solution.py:66
  43.8 1.1 fusion.44
  44.9 0.8 convert_reduce_fusion.2
  45.6 1.2 fusion.45
  46.9 1.1 fusion.44
  48.0 0.8 convert_reduce_fusion.2
  48.8 1.2 fusion.45
  50.0 1.1 fusion.44
  51.1 0.8 convert_reduce_fusion.2
  51.9 1.2 fusion.45
  53.1 1.1 fusion.44
  54.2 0.8 convert_reduce_fusion.2
  55.0 1.2 fusion.45
  56.2 1.1 fusion.44
  57.4 0.8 convert_reduce_fusion.2
  58.1 1.2 fusion.45
  59.4 1.1 fusion.44
  60.5 0.8 convert_reduce_fusion.2
  61.2 1.2 fusion.45
  62.5 1.1 fusion.44
  63.6 0.8 convert_reduce_fusion.2
  64.4 1.2 fusion.45
  65.6 1.1 fusion.44
  66.7 0.8 convert_reduce_fusion.2
  67.5 1.2 fusion.45
  68.7 0.0 copy-start
  68.7 1.0 copy-done
  69.7 0.0 all-reduce.3.cloned.1.call-update
  69.7 0.0 all-reduce.5.cloned.1.call-start
  69.8 34.6 %all-reduce.3.cloned.1.call-done = f32[16,16384]{1,0:T(8,128)} async-done(((f32[16,16384]{1,0:T(8,128)}), f32[16,16384]{1,0:T(8,128)}) %all-reduce.3.cloned.1.call-update) | async-done | bytes 1048592 | tf_op jit(solution)/shard_map/psum | solution.py:69
  104.4 0.0 all-reduce.5.cloned.1.call-update
  104.4 42.9 %all-reduce.5.cloned.1.call-done = f32[16,16384]{1,0:T(8,128)} async-done(((f32[16,16384]{1,0:T(8,128)}), f32[16,16384]{1,0:T(8,128)}) %all-reduce.5.cloned.1.call-update) | async-done | bytes 1048592 | tf_op jit(solution)/shard_map/psum | solution.py:69
  147.3 2.3 %broadcast_multiply_fusion = f32[16,16384]{1,0:T(8,128)} fusion(f32[16,16384]{1,0:T(8,128)} %all-reduce.5.cloned.1.call-done, f32[16]{0:T(128)S(1)} %get-tuple-element.358), kind=kLoop, calls=%fused_computation.28 | loop fusion | flops 262144 | bytes 2097216 | tf_op jit(solution)/shard_map/mul | solution.py:71
  (21 shorter events, 0.1 us)
Async XLA Ops:
  6.5 4.7 %copy-start.2 = (bf16[8,16384]{1,0:T(8,128)(2,1)S(1)}, bf16[8,16384]{1,0:T(8,128)(2,1)}, u32[]{:S(2)}) copy-start(bf16[8,16384]{1,0:T(8,128)(2,1)} %param.14) | copy-start | bytes 786436
  6.5 97.8 %all-reduce.3.cloned.1.call-start = ((), (), s32[]{:S(2)}) async-start(), calls=%async_computation | async-start | bytes 2097152 | tf_op jit(solution)/shard_map/psum | solution.py:69
  11.3 32.4 %copy-start.1 = (bf16[16,512]{1,0:T(8,128)(2,1)S(1)}, bf16[16,512]{1,0:T(8,128)(2,1)}, u32[]{:S(2)}) copy-start(bf16[16,512]{1,0:T(8,128)(2,1)} %param.10) | copy-start | bytes 49156
  68.7 1.0 copy-start
  69.7 77.5 %all-reduce.5.cloned.1.call-start = ((), (), s32[]{:S(2)}) async-start(), calls=%async_computation.1 | async-start | bytes 2097152 | tf_op jit(solution)/shard_map/psum | solution.py:69
Sparse Core Ops, SparseCore 0:
  69.9 34.4 all-reduce.2
  106.7 40.5 all-reduce.4
